TPU v7x, 128 devices: a whole 4x4x4 slice. The times are simulated.
128 devices in a mesh: store: 8 (over z, core), mp: 16 (over y, x).
Axes of the slice: x: 4, y: 4, z: 4, core: 2. Of those that a mesh axis runs over, the one named last changes fastest.
Arguments:
- tokens: bfloat16 [2048, 6144], P('store', 'mp'), may hold values from -6 to 6
- gain: float32 [6144], replicated, may hold values from 0.1 to 1.9
- base_projection_weight: bfloat16 [6144, 6144], P(None, 'mp'), may hold values from -0.078125 to 0.078125
- adapter_down_weight: bfloat16 [64, 64, 6144], P('store', None, 'mp'), may hold values from -0.078125 to 0.078125
- adapter_up_weight: bfloat16 [64, 64, 6144], P('store', None, 'mp'), may hold values from -0.75 to 0.75
- plan: int32 [8, 4], replicated, may hold values from 0 to 63, as said below
- target: int32 [2048, 1], P('store'), may hold values from 0 to 7; in each aligned block of 256 rows (0 to 255, 256 to 511, ...) at most 64 rows name the same one
- slot: int32 [2048], P('store'), may hold values from 0 to 11
Outputs:
- hidden_out: bfloat16 [2048, 6144], P('store', 'mp')
Inputs may be any that keep to these rules, and one draw needn't show every extreme that they name: plan[g, r] is an adapter owned by a store group other than g; adapter a is owned by group a // 8. `target`: among the 256 rows of one store group at most 64 name the same group, a bound that some block reaches.
All inputs are finite; a program needn't handle non-finite values.
Results may differ from a plain program's by a relative error of at most 0.0063.
Values may be sent and summed in bfloat16 or wider, within the bound.
A program may use at most 64 MiB of HBM per device.

v0:
```python
import jax
import jax.numpy as jnp
from jax import lax
from jax.sharding import PartitionSpec as P

STEPS = 4
CAP = 64
adapter_scale = 0.5


def local(
    tokens, gain, base_projection_weight, adapter_down_weight, adapter_up_weight, plan, target, slot
):
    store_count = lax.axis_size("store")
    group = lax.axis_index("store")
    owned_adapters = adapter_down_weight.shape[0]
    rank_position = adapter_down_weight.shape[1]
    width_portion = adapter_down_weight.shape[2]
    replica_count = plan.shape[1]
    n_slots = owned_adapters + replica_count
    flattened_down = adapter_down_weight.reshape(owned_adapters, rank_position * width_portion)
    flattened_up = adapter_up_weight.reshape(owned_adapters, rank_position * width_portion)
    own_plan = lax.dynamic_slice_in_dim(plan, group, 1, 0)[0]
    pieces = (
        lax.all_gather(flattened_down, "store", axis=0, tiled=True),
        lax.all_gather(flattened_up, "store", axis=0, tiled=True),
    )
    count = pieces[0].shape[0]
    select = (own_plan[:, None] == jnp.arange(count, dtype=jnp.int32)[None, :]).astype(jnp.bfloat16)
    replica_down_factor = jnp.dot(select, pieces[0], preferred_element_type=jnp.float32)
    replica_up_factor = jnp.dot(select, pieces[1], preferred_element_type=jnp.float32)
    host_down = jnp.concatenate(
        [
            adapter_down_weight,
            replica_down_factor.astype(jnp.bfloat16).reshape(
                replica_count, rank_position, width_portion
            ),
        ],
        0,
    )
    host_down = host_down.reshape(n_slots * rank_position, width_portion)
    host_up = jnp.concatenate(
        [
            adapter_up_weight,
            replica_up_factor.astype(jnp.bfloat16).reshape(
                replica_count, rank_position, width_portion
            ),
        ],
        0,
    )
    host_up = host_up.reshape(n_slots * rank_position, width_portion)
    target_group = target[:, 0]
    member = (target_group[:, None] == jnp.arange(store_count, dtype=jnp.int32)[None, :]).astype(
        jnp.int32
    )
    earlier = jnp.cumsum(member, axis=0) - member
    bucket_place = jnp.sum(earlier * member, axis=1)
    row_index = target_group * CAP + bucket_place
    slot_buffer = (
        jnp.full((store_count * CAP,), -1, jnp.int32)
        .at[row_index]
        .set(slot)
        .reshape(store_count, CAP)
    )
    state = tokens
    column_start = lax.axis_index("mp") * width_portion
    for step in range(STEPS):
        whole = lax.all_gather(state, "mp", axis=1, tiled=True)
        values = whole.astype(jnp.float32)
        mean_sq = jnp.mean(values * values, axis=1, keepdims=True)
        normed = (values * lax.rsqrt(mean_sq + 1e-05) * gain[None, :]).astype(jnp.bfloat16)
        mine = lax.dynamic_slice_in_dim(normed, column_start, width_portion, 1)
        row_buffer = (
            jnp.zeros((store_count * CAP, width_portion), jnp.bfloat16).at[row_index].set(mine)
        )
        row_buffer = row_buffer.reshape(store_count, CAP, width_portion)
        rows = lax.all_to_all(row_buffer, "store", split_axis=0, concat_axis=0, tiled=True)
        slots_in = lax.all_to_all(slot_buffer, "store", split_axis=0, concat_axis=0, tiled=True)
        senders, adapter_count = slots_in.shape
        total_rows = senders * adapter_count
        flat_rows = rows.reshape(total_rows, width_portion)
        partial_value = lax.dot_general(
            flat_rows, host_down, (((1,), (1,)), ((), ())), preferred_element_type=jnp.float32
        )
        selected_adapter = (
            slots_in.reshape(total_rows)[:, None] == jnp.arange(n_slots, dtype=jnp.int32)[None, :]
        )
        partial_value = jnp.sum(
            partial_value.reshape(total_rows, n_slots, rank_position)
            * selected_adapter[:, :, None].astype(jnp.float32),
            axis=1,
        )
        summed_share = lax.psum_scatter(
            partial_value, "mp", scatter_dimension=0, tiled=True
        ).astype(jnp.bfloat16)
        inner = lax.all_gather(summed_share, "mp", axis=0, tiled=True)
        spread_rows = (
            selected_adapter[:, :, None].astype(jnp.bfloat16) * inner[:, None, :]
        ).reshape(total_rows, n_slots * rank_position)
        outer = jnp.dot(spread_rows, host_up, preferred_element_type=jnp.float32)
        outer = (
            (adapter_scale * outer)
            .astype(jnp.bfloat16)
            .reshape(senders, adapter_count, width_portion)
        )
        returned = lax.all_to_all(outer, "store", split_axis=0, concat_axis=0, tiled=True)
        delta = returned.reshape(store_count * CAP, width_portion)[row_index]
        base = jnp.dot(normed, base_projection_weight, preferred_element_type=jnp.float32)
        state = (state.astype(jnp.float32) + base + delta.astype(jnp.float32)).astype(jnp.bfloat16)
    return state


def solution(mesh):
    return jax.shard_map(
        local,
        mesh=mesh,
        in_specs=(
            P("store", "mp"),
            P(),
            P(None, "mp"),
            P("store", None, "mp"),
            P("store", None, "mp"),
            P(),
            P("store", None),
            P("store"),
        ),
        out_specs=P("store", "mp"),
        check_vma=False,
    )
```

profile of v0, /device:TPU:1, one launch (start us, length us, event | category | flops | bytes accessed | tf_op | source)
XLA Modules:
  0.0 813.4 jit_solution(17470650637500841050)
XLA Ops:
  16.6 6.8 all-to-all-start
  29.9 33.1 %all-gather.7.cloned.1.call-done = bf16[256,6144]{1,0:T(8,128)(2,1)} async-done(((bf16[256,384]{1,0:T(8,128)(2,1)}), bf16[256,6144]{1,0:T(8,128)(2,1)}) %all-gather.7.cloned.1.call-update) | async-done | bytes 3145744 | tf_op jit(solution)/shard_map/all_gather | solution.py:68
  69.9 6.5 all-to-all-start.1
  76.4 21.6 %all-gather.9.cloned.1.call-done = bf16[64,24576]{1,0:T(8,128)(2,1)} async-done(((bf16[8,24576]{1,0:T(8,128)(2,1)}), bf16[64,24576]{1,0:T(8,128)(2,1)}) %all-gather.9.cloned.1.call-update) | async-done | bytes 3145744 | tf_op jit(solution)/shard_map/all_gather | solution.py:25
  105.3 20.9 %all-gather.11.cloned.1.call-done = bf16[64,24576]{1,0:T(8,128)(2,1)} async-done(((bf16[8,24576]{1,0:T(8,128)(2,1)}), bf16[64,24576]{1,0:T(8,128)(2,1)}) %all-gather.11.cloned.1.call-update) | async-done | bytes 3145744 | tf_op jit(solution)/shard_map/all_gather | solution.py:26
  129.4 70.7 %reduce-scatter.13.cloned.1.call-done = f32[32,64]{1,0:T(8,128)} async-done(((f32[512,64]{1,0:T(8,128)}), f32[32,64]{1,0:T(8,128)}) %reduce-scatter.13.cloned.1.call-update) | async-done | bytes 8208 | tf_op jit(solution)/shard_map/reduce_scatter | solution.py:93
  200.9 17.0 %all_gather.32 = bf16[512,64]{1,0:T(8,128)(2,1)S(1)} all-gather(bf16[32,64]{1,0:T(8,128)(2,1)S(1)} %convert_element_type.128), channel_id=1, replica_groups=mesh['store'=8,'mp'=16] {'mp'}, dimensions={0}, use_global_device_ids=true | all-gather | bytes 69632 | tf_op jit(solution)/shard_map/all_gather | solution.py:96
  220.4 12.9 %all-to-all-start.2 = ((bf16[8,64,384]{2,1,0:T(8,128)(2,1)}), bf16[8,64,384]{2,1,0:T(8,128)(2,1)S(1)}, u32[]{:S(2)}, u32[]{:S(2)}) async-start(bf16[8,64,384]{2,1,0:T(8,128)(2,1)} %bitcast.115), calls=%async_computation.2 | async-start | bytes 786432 | tf_op jit(solution)/shard_map/all_to_all | solution.py:106
  233.2 7.7 all-to-all-done.2
  248.0 47.6 %all-gather.13.cloned.1.call-done = bf16[256,6144]{1,0:T(8,128)(2,1)} async-done(((bf16[256,384]{1,0:T(8,128)(2,1)}), bf16[256,6144]{1,0:T(8,128)(2,1)}) %all-gather.13.cloned.1.call-update) | async-done | bytes 3145744 | tf_op jit(solution)/shard_map/all_gather | solution.py:68
  301.2 14.3 %all_to_all.52 = bf16[8,64,384]{2,1,0:T(8,128)(2,1)S(1)} all-to-all(bf16[8,64,384]{2,1,0:T(8,128)(2,1)S(1)} %bitcast.110), channel_id=1, replica_groups=mesh['store'=8,'mp'=16] {'store'}, dimensions={0} | all-to-all | bytes 786432 | tf_op jit(solution)/shard_map/all_to_all | solution.py:77
  318.1 69.2 %reduce-scatter.15.cloned.1.call-done = f32[32,64]{1,0:T(8,128)} async-done(((f32[512,64]{1,0:T(8,128)}), f32[32,64]{1,0:T(8,128)}) %reduce-scatter.15.cloned.1.call-update) | async-done | bytes 8208 | tf_op jit(solution)/shard_map/reduce_scatter | solution.py:93
  388.0 17.0 %all_gather.35 = bf16[512,64]{1,0:T(8,128)(2,1)S(1)} all-gather(bf16[32,64]{1,0:T(8,128)(2,1)S(1)} %convert_element_type.136), channel_id=1, replica_groups=mesh['store'=8,'mp'=16] {'mp'}, dimensions={0}, use_global_device_ids=true | all-gather | bytes 69632 | tf_op jit(solution)/shard_map/all_gather | solution.py:96
  406.7 20.7 %all_to_all.53 = bf16[8,64,384]{2,1,0:T(8,128)(2,1)S(1)} all-to-all(bf16[8,64,384]{2,1,0:T(8,128)(2,1)S(1)} %bitcast.119), channel_id=1, replica_groups=mesh['store'=8,'mp'=16] {'store'}, dimensions={0} | all-to-all | bytes 786432 | tf_op jit(solution)/shard_map/all_to_all | solution.py:106
  434.4 47.4 %all-gather.15.cloned.1.call-done = bf16[256,6144]{1,0:T(8,128)(2,1)} async-done(((bf16[256,384]{1,0:T(8,128)(2,1)}), bf16[256,6144]{1,0:T(8,128)(2,1)}) %all-gather.15.cloned.1.call-update) | async-done | bytes 3145744 | tf_op jit(solution)/shard_map/all_gather | solution.py:68
  487.3 14.3 %all_to_all.54 = bf16[8,64,384]{2,1,0:T(8,128)(2,1)S(1)} all-to-all(bf16[8,64,384]{2,1,0:T(8,128)(2,1)S(1)} %bitcast.111), channel_id=1, replica_groups=mesh['store'=8,'mp'=16] {'store'}, dimensions={0} | all-to-all | bytes 786432 | tf_op jit(solution)/shard_map/all_to_all | solution.py:77
  504.2 69.2 %reduce-scatter.17.cloned.1.call-done = f32[32,64]{1,0:T(8,128)} async-done(((f32[512,64]{1,0:T(8,128)}), f32[32,64]{1,0:T(8,128)}) %reduce-scatter.17.cloned.1.call-update) | async-done | bytes 8208 | tf_op jit(solution)/shard_map/reduce_scatter | solution.py:93
  574.1 17.0 %all_gather.37 = bf16[512,64]{1,0:T(8,128)(2,1)S(1)} all-gather(bf16[32,64]{1,0:T(8,128)(2,1)S(1)} %convert_element_type.143), channel_id=1, replica_groups=mesh['store'=8,'mp'=16] {'mp'}, dimensions={0}, use_global_device_ids=true | all-gather | bytes 69632 | tf_op jit(solution)/shard_map/all_gather | solution.py:96
  592.9 20.7 %all_to_all.55 = bf16[8,64,384]{2,1,0:T(8,128)(2,1)S(1)} all-to-all(bf16[8,64,384]{2,1,0:T(8,128)(2,1)S(1)} %bitcast.121), channel_id=1, replica_groups=mesh['store'=8,'mp'=16] {'store'}, dimensions={0} | all-to-all | bytes 786432 | tf_op jit(solution)/shard_map/all_to_all | solution.py:106
  620.5 47.4 %all-gather.17.cloned.1.call-done = bf16[256,6144]{1,0:T(8,128)(2,1)} async-done(((bf16[256,384]{1,0:T(8,128)(2,1)}), bf16[256,6144]{1,0:T(8,128)(2,1)}) %all-gather.17.cloned.1.call-update) | async-done | bytes 3145744 | tf_op jit(solution)/shard_map/all_gather | solution.py:68
  673.5 14.3 %all_to_all.56 = bf16[8,64,384]{2,1,0:T(8,128)(2,1)S(1)} all-to-all(bf16[8,64,384]{2,1,0:T(8,128)(2,1)S(1)} %bitcast.109), channel_id=1, replica_groups=mesh['store'=8,'mp'=16] {'store'}, dimensions={0} | all-to-all | bytes 786432 | tf_op jit(solution)/shard_map/all_to_all | solution.py:77
  690.3 69.2 %reduce-scatter.19.cloned.1.call-done = f32[32,64]{1,0:T(8,128)} async-done(((f32[512,64]{1,0:T(8,128)}), f32[32,64]{1,0:T(8,128)}) %reduce-scatter.19.cloned.1.call-update) | async-done | bytes 8208 | tf_op jit(solution)/shard_map/reduce_scatter | solution.py:93
  760.2 17.0 %all_gather.39 = bf16[512,64]{1,0:T(8,128)(2,1)S(1)} all-gather(bf16[32,64]{1,0:T(8,128)(2,1)S(1)} %convert_element_type.150), channel_id=1, replica_groups=mesh['store'=8,'mp'=16] {'mp'}, dimensions={0}, use_global_device_ids=true | all-gather | bytes 69632 | tf_op jit(solution)/shard_map/all_gather | solution.py:96
  779.0 20.7 %all_to_all.57 = bf16[8,64,384]{2,1,0:T(8,128)(2,1)S(1)} all-to-all(bf16[8,64,384]{2,1,0:T(8,128)(2,1)S(1)} %bitcast.117), channel_id=1, replica_groups=mesh['store'=8,'mp'=16] {'store'}, dimensions={0} | all-to-all | bytes 786432 | tf_op jit(solution)/shard_map/all_to_all | solution.py:106
  (115 shorter events, 96.5 us)
Async XLA Ops:
  6.5 19.4 %copy-start = (s32[8,4]{0,1:T(4,128)S(1)}, s32[8,4]{0,1:T(4,128)}, u32[]{:S(2)}) copy-start(s32[8,4]{0,1:T(4,128)} %param.13) | copy-start | bytes 388
  6.5 18.6 %copy-start.5 = (bf16[8,64,384]{2,1,0:T(8,128)(2,1)S(1)}, bf16[8,64,384]{2,1,0:T(8,128)(2,1)}, u32[]{:S(2)}) copy-start(bf16[8,64,384]{2,1,0:T(8,128)(2,1)} %param.12) | copy-start | bytes 1179652
  6.5 56.5 %all-gather.7.cloned.1.call-start = ((), (), s32[]{:S(2)}) async-start(), calls=%async_computation.13 | async-start | bytes 3342336 | tf_op jit(solution)/shard_map/all_gather | solution.py:68
  7.3 90.7 %all-gather.9.cloned.1.call-start = ((), (), s32[]{:S(2)}) async-start(), calls=%async_computation.14 | async-start | bytes 3538944 | tf_op jit(solution)/shard_map/all_gather | solution.py:25
  9.3 116.9 %all-gather.11.cloned.1.call-start = ((), (), s32[]{:S(2)}) async-start(), calls=%async_computation.15 | async-start | bytes 3538944 | tf_op jit(solution)/shard_map/all_gather | solution.py:26
  16.6 11.4 %all-to-all-start = ((s32[8,1,64]{2,1,0:T(1,128)}), s32[8,1,64]{2,1,0:T(1,128)S(1)}, u32[]{:S(2)}, u32[]{:S(2)}) async-start(s32[8,1,64]{2,1,0:T(1,128)} %all_to_all.33), calls=%async_computation | async-start | bytes 8192 | tf_op jit(solution)/shard_map/all_to_all | solution.py:78
  63.0 2.8 copy-start.1
  69.9 31.3 %all-to-all-start.1 = ((bf16[8,64,384]{2,1,0:T(8,128)(2,1)}), bf16[8,64,384]{2,1,0:T(8,128)(2,1)S(1)}, u32[]{:S(2)}, u32[]{:S(2)}) async-start(bf16[8,64,384]{2,1,0:T(8,128)(2,1)} %bitcast.6), calls=%async_computation.1 | async-start | bytes 786432 | tf_op jit(solution)/shard_map/all_to_all | solution.py:77
  76.4 123.8 %reduce-scatter.13.cloned.1.call-start = ((), (), s32[]{:S(2)}) async-start(), calls=%async_computation.19 | async-start | bytes 278528 | tf_op jit(solution)/shard_map/reduce_scatter | solution.py:93
  103.5 114.4 %copy-start.9 = (bf16[512,12]{0,1:T(8,128)(2,1)S(1)}, bf16[512,12]{0,1:T(8,128)(2,1)}, u32[]{:S(2)}) copy-start(bf16[512,12]{0,1:T(8,128)(2,1)} %get-tuple-element.5) | copy-start | bytes 36868
  220.4 20.6 %all-to-all-start.2 = ((bf16[8,64,384]{2,1,0:T(8,128)(2,1)}), bf16[8,64,384]{2,1,0:T(8,128)(2,1)S(1)}, u32[]{:S(2)}, u32[]{:S(2)}) async-start(bf16[8,64,384]{2,1,0:T(8,128)(2,1)} %bitcast.115), calls=%async_computation.2 | async-start | bytes 786432 | tf_op jit(solution)/shard_map/all_to_all | solution.py:106
  233.2 62.4 %all-gather.13.cloned.1.call-start = ((), (), s32[]{:S(2)}) async-start(), calls=%async_computation.16 | async-start | bytes 3342336 | tf_op jit(solution)/shard_map/all_gather | solution.py:68
  247.8 50.6 %copy-start.6 = (f32[6144]{0:T(1024)S(1)}, f32[6144]{0:T(1024)}, u32[]{:S(2)}) copy-start(f32[6144]{0:T(1024)} %param.9) | copy-start | bytes 73732
  247.8 139.4 %reduce-scatter.15.cloned.1.call-start = ((), (), s32[]{:S(2)}) async-start(), calls=%async_computation.20 | async-start | bytes 278528 | tf_op jit(solution)/shard_map/reduce_scatter | solution.py:93
  295.6 2.8 copy-start.2
  315.5 89.5 %copy-start.10 = (bf16[512,12]{0,1:T(8,128)(2,1)S(1)}, bf16[512,12]{0,1:T(8,128)(2,1)}, u32[]{:S(2)}) copy-start(bf16[512,12]{0,1:T(8,128)(2,1)} %get-tuple-element.5) | copy-start | bytes 36868
  318.0 163.8 %all-gather.15.cloned.1.call-start = ((), (), s32[]{:S(2)}) async-start(), calls=%async_computation.17 | async-start | bytes 3342336 | tf_op jit(solution)/shard_map/all_gather | solution.py:68
  434.3 50.3 %copy-start.7 = (f32[6144]{0:T(1024)S(1)}, f32[6144]{0:T(1024)}, u32[]{:S(2)}) copy-start(f32[6144]{0:T(1024)} %param.9) | copy-start | bytes 73732
  434.3 139.1 %reduce-scatter.17.cloned.1.call-start = ((), (), s32[]{:S(2)}) async-start(), calls=%async_computation.21 | async-start | bytes 278528 | tf_op jit(solution)/shard_map/reduce_scatter | solution.py:93
  501.6 89.5 %copy-start.11 = (bf16[512,12]{0,1:T(8,128)(2,1)S(1)}, bf16[512,12]{0,1:T(8,128)(2,1)}, u32[]{:S(2)}) copy-start(bf16[512,12]{0,1:T(8,128)(2,1)} %get-tuple-element.5) | copy-start | bytes 36868
  504.2 163.8 %all-gather.17.cloned.1.call-start = ((), (), s32[]{:S(2)}) async-start(), calls=%async_computation.18 | async-start | bytes 3342336 | tf_op jit(solution)/shard_map/all_gather | solution.py:68
  620.4 50.3 %copy-start.8 = (f32[6144]{0:T(1024)S(1)}, f32[6144]{0:T(1024)}, u32[]{:S(2)}) copy-start(f32[6144]{0:T(1024)} %param.9) | copy-start | bytes 73732
  620.4 139.1 %reduce-scatter.19.cloned.1.call-start = ((), (), s32[]{:S(2)}) async-start(), calls=%async_computation.22 | async-start | bytes 278528 | tf_op jit(solution)/shard_map/reduce_scatter | solution.py:93
  687.8 89.5 %copy-start.12 = (bf16[512,12]{0,1:T(8,128)(2,1)S(1)}, bf16[512,12]{0,1:T(8,128)(2,1)}, u32[]{:S(2)}) copy-start(bf16[512,12]{0,1:T(8,128)(2,1)} %get-tuple-element.5) | copy-start | bytes 36868
  (2 other events, 5.7 us)
Sparse Core Ops, SparseCore 0:
  9.4 53.5 all-gather.6
  64.7 33.2 all-gather.8
  99.7 26.5 all-gather.10
  129.3 70.8 reduce-scatter.12
  247.9 47.6 all-gather.12
  318.1 69.0 reduce-scatter.14
  434.4 47.3 all-gather.14
  504.3 69.0 reduce-scatter.16
  620.6 47.3 all-gather.16
  690.4 69.0 reduce-scatter.18
where the time goes:
time: 815 us; the launch traced here: 813 us
  waiting for transfers between devices  507 us (62%)
  blocking collectives  173 us (21%)
  matrix products  39.8 us (5%)
  local copies, waits for them, and re-layouts  30.5 us (4%)
  starting transfers between devices  26.6 us (3%)
  other arithmetic  23 us (3%)
  between operations  13.8 us (2%)
    reduce_scatter x4, waiting for transfers between devices, local(): lax.psum_scatter(partial_value, 'mp', scatter_dimension=0, tiled=True)  278 us
    all_gather x4, waiting for transfers between devices, local(): whole = lax.all_gather(state, 'mp', axis=1, tiled=True)  176 us
    all_gather x4, blocking collectives, local(): inner = lax.all_gather(summed_share, 'mp', axis=0, tiled=True)  67.8 us
    all_to_all x3, blocking collectives, local(): lax.all_to_all(outer, 'store', split_axis=0, concat_axis=0, tiled=True)  62.2 us
    all_to_all x3, blocking collectives, local(): lax.all_to_all(row_buffer, 'store', split_axis=0, concat_axis=0, tiled=True)  42.9 us
    all_gather x1, waiting for transfers between devices, local(): lax.all_gather(flattened_down, 'store', axis=0, tiled=True)  21.6 us
    all_gather x1, waiting for transfers between devices, local(): lax.all_gather(flattened_up, 'store', axis=0, tiled=True)  20.9 us
    dot_general x4, matrix products, local(): jnp.dot(normed, base_projection_weight, preferred_element_type=jnp.float32)  20.1 us
  transfers between devices with their start and end apart: 13, of which 12 were waited for; matrix products, arithmetic and copies ran while one was open for 4% of the time, Pallas kernels for 0%

commit v1 on v0

--- a/solution.py
+++ b/solution.py
@@ -6,6 +6,12 @@
 STEPS = 4
 CAP = 64
 adapter_scale = 0.5
+
+
+def tiled_gather(x, axis, dim):
+    peers = lax.axis_size(axis)
+    repeats = [peers if d == dim else 1 for d in range(x.ndim)]
+    return lax.all_to_all(jnp.tile(x, repeats), axis, split_axis=dim, concat_axis=dim, tiled=True)
 
 
 def local(
@@ -65,7 +71,7 @@
     state = tokens
     column_start = lax.axis_index("mp") * width_portion
     for step in range(STEPS):
-        whole = lax.all_gather(state, "mp", axis=1, tiled=True)
+        whole = tiled_gather(state, "mp", 1)
         values = whole.astype(jnp.float32)
         mean_sq = jnp.mean(values * values, axis=1, keepdims=True)
         normed = (values * lax.rsqrt(mean_sq + 1e-05) * gain[None, :]).astype(jnp.bfloat16)

time: 815 us -> 772 us (0.947)
  waiting for transfers between devices: 507 us -> 324 us
  blocking collectives: 173 us -> 306 us
  local copies, waits for them, and re-layouts: 30.5 us -> 51.2 us
  other arithmetic: 23 us -> 13.7 us
    all_gather x4 -> x0, waiting for transfers between devices: 176 us -> none  [local(): whole = lax.all_gather(state, 'mp', axis=1, tiled=True)]
    all_to_all x0 -> x4, blocking collectives: none -> 139 us  [the longest x3 127 us: tiled_gather(): lax.all_to_all(jnp.tile(x, repeats), axis, split_axis=dim, concat_axis=di...]
    all_to_all x1, waiting for transfers between devices: 1.86 us -> 42.7 us  [tiled_gather(): lax.all_to_all(jnp.tile(x, repeats), axis, split_axis=dim, concat_axis=di...]
    all_gather x1, waiting for transfers between devices: 21.6 us -> 0.01 us  [local(): lax.all_gather(flattened_down, 'store', axis=0, tiled=True)]
    all_gather x1, waiting for transfers between devices: 20.9 us -> 0.02 us  [local(): lax.all_gather(flattened_up, 'store', axis=0, tiled=True)]
    all_to_all x0 -> x4, local copies, waits for them, and re-layouts: none -> 12.7 us  [tiled_gather(): lax.all_to_all(jnp.tile(x, repeats), axis, split_axis=dim, concat_axis=di...]
    reduce_scatter x4, waiting for transfers between devices: 278 us -> 268 us  [local(): lax.psum_scatter(partial_value, 'mp', scatter_dimension=0, tiled=True)]
  transfers between devices with their start and end apart: 13 -> 9, of which waited for: 12 -> 7; matrix products, arithmetic and copies ran while one was open for 4% -> 3% of each run, Pallas kernels for 0% -> 0%
where the time goes in v1:
time: 772 us; the launch traced here: 770 us
  waiting for transfers between devices  324 us (42%)
  blocking collectives  306 us (40%)
  local copies, waits for them, and re-layouts  51.2 us (7%)
  matrix products  36.5 us (5%)
  starting transfers between devices  25.1 us (3%)
  between operations  14 us (2%)
  other arithmetic  13.7 us (2%)
    reduce_scatter x4, waiting for transfers between devices, local(): lax.psum_scatter(partial_value, 'mp', scatter_dimension=0, tiled=True)  268 us
    all_to_all x3, blocking collectives, tiled_gather(): lax.all_to_all(jnp.tile(x, repeats), axis, split_axis=dim, concat_axis=di...  127 us
    all_gather x4, blocking collectives, local(): inner = lax.all_gather(summed_share, 'mp', axis=0, tiled=True)  68 us
    all_to_all x3, blocking collectives, local(): lax.all_to_all(outer, 'store', split_axis=0, concat_axis=0, tiled=True)  62.2 us
    all_to_all x1, waiting for transfers between devices, tiled_gather(): lax.all_to_all(jnp.tile(x, repeats), axis, split_axis=dim, concat_axis=di...  42.7 us
    all_to_all x3, blocking collectives, local(): lax.all_to_all(row_buffer, 'store', split_axis=0, concat_axis=0, tiled=True)  37.5 us
    dot_general x4, matrix products, local(): jnp.dot(normed, base_projection_weight, preferred_element_type=jnp.float32)  17.9 us
    unnamed x66, local copies, waits for them, and re-layouts  15.6 us
  transfers between devices with their start and end apart: 9, of which 7 were waited for; matrix products, arithmetic and copies ran while one was open for 3% of the time, Pallas kernels for 0%

profile of v1, /device:TPU:1, one launch (start us, length us, event | category | flops | bytes accessed | tf_op | source)
XLA Modules:
  0.0 770.5 jit_solution(13063073132219681290)
XLA Ops:
  13.2 11.2 %all_to_all.76 = s32[8,1,64]{2,1,0:T(1,128)S(1)} all-to-all(s32[8,1,64]{2,1,0:T(1,128)S(1)} %all_to_all.50), channel_id=1, replica_groups=mesh['store'=8,'mp'=16] {'store'}, dimensions={0} | all-to-all | bytes 4096 | tf_op jit(solution)/shard_map/all_to_all | solution.py:84
  27.3 6.9 all-to-all-start
  38.4 42.7 %all-to-all-done = bf16[256,16,384]{2,0,1:T(8,128)(2,1)} async-done(((bf16[256,16,384]{2,0,1:T(8,128)(2,1)}), bf16[256,16,384]{2,0,1:T(8,128)(2,1)}, u32[]{:S(2)}, u32[]{:S(2)}) %all-to-all-start) | async-done | bytes 3145760 | tf_op jit(solution)/shard_map/all_to_all | solution.py:14
  90.3 5.1 all-to-all-start.2
  97.9 5.2 all-to-all-done.2
  107.8 65.7 %reduce-scatter.13.cloned.1.call-done = f32[32,64]{1,0:T(8,128)} async-done(((f32[512,64]{1,0:T(8,128)}), f32[32,64]{1,0:T(8,128)}) %reduce-scatter.13.cloned.1.call-update) | async-done | bytes 8208 | tf_op jit(solution)/shard_map/reduce_scatter | solution.py:99
  174.3 17.0 %all_gather.19 = bf16[512,64]{1,0:T(8,128)(2,1)S(1)} all-gather(bf16[32,64]{1,0:T(8,128)(2,1)S(1)} %convert_element_type.154), channel_id=1, replica_groups=mesh['store'=8,'mp'=16] {'mp'}, dimensions={0}, use_global_device_ids=true | all-gather | bytes 69632 | tf_op jit(solution)/shard_map/all_gather | solution.py:102
  193.9 12.9 %all-to-all-start.3 = ((bf16[8,64,384]{2,1,0:T(8,128)(2,1)}), bf16[8,64,384]{2,1,0:T(8,128)(2,1)S(1)}, u32[]{:S(2)}, u32[]{:S(2)}) async-start(bf16[8,64,384]{2,1,0:T(8,128)(2,1)} %bitcast.139), calls=%async_computation.3 | async-start | bytes 786432 | tf_op jit(solution)/shard_map/all_to_all | solution.py:112
  206.8 7.7 all-to-all-done.3
  221.4 42.2 %all_to_all.77 = bf16[256,16,384]{2,0,1:T(8,128)(2,1)} all-to-all(bf16[256,16,384]{2,0,1:T(8,128)(2,1)S(1)} %tile.9), channel_id=1, replica_groups=mesh['store'=8,'mp'=16] {'mp'}, dimensions={1} | all-to-all | bytes 6291456 | tf_op jit(solution)/shard_map/all_to_all | solution.py:14
  272.1 12.7 %all_to_all.78 = bf16[8,64,384]{2,1,0:T(8,128)(2,1)S(1)} all-to-all(bf16[8,64,384]{2,1,0:T(8,128)(2,1)S(1)} %bitcast.134), channel_id=1, replica_groups=mesh['store'=8,'mp'=16] {'store'}, dimensions={0} | all-to-all | bytes 786432 | tf_op jit(solution)/shard_map/all_to_all | solution.py:83
  287.4 67.4 %reduce-scatter.15.cloned.1.call-done = f32[32,64]{1,0:T(8,128)} async-done(((f32[512,64]{1,0:T(8,128)}), f32[32,64]{1,0:T(8,128)}) %reduce-scatter.15.cloned.1.call-update) | async-done | bytes 8208 | tf_op jit(solution)/shard_map/reduce_scatter | solution.py:99
  355.6 16.9 %all_gather.21 = bf16[512,64]{1,0:T(8,128)(2,1)S(1)} all-gather(bf16[32,64]{1,0:T(8,128)(2,1)S(1)} %convert_element_type.164), channel_id=1, replica_groups=mesh['store'=8,'mp'=16] {'mp'}, dimensions={0}, use_global_device_ids=true | all-gather | bytes 69632 | tf_op jit(solution)/shard_map/all_gather | solution.py:102
  374.5 20.7 %all_to_all.79 = bf16[8,64,384]{2,1,0:T(8,128)(2,1)S(1)} all-to-all(bf16[8,64,384]{2,1,0:T(8,128)(2,1)S(1)} %bitcast.143), channel_id=1, replica_groups=mesh['store'=8,'mp'=16] {'store'}, dimensions={0} | all-to-all | bytes 786432 | tf_op jit(solution)/shard_map/all_to_all | solution.py:112
  402.0 42.6 %all_to_all.80 = bf16[256,16,384]{2,0,1:T(8,128)(2,1)} all-to-all(bf16[256,16,384]{2,0,1:T(8,128)(2,1)S(1)} %tile.10), channel_id=1, replica_groups=mesh['store'=8,'mp'=16] {'mp'}, dimensions={1} | all-to-all | bytes 6291456 | tf_op jit(solution)/shard_map/all_to_all | solution.py:14
  453.1 12.4 %all_to_all.81 = bf16[8,64,384]{2,1,0:T(8,128)(2,1)S(1)} all-to-all(bf16[8,64,384]{2,1,0:T(8,128)(2,1)S(1)} %bitcast.135), channel_id=1, replica_groups=mesh['store'=8,'mp'=16] {'store'}, dimensions={0} | all-to-all | bytes 786432 | tf_op jit(solution)/shard_map/all_to_all | solution.py:83
  468.1 67.4 %reduce-scatter.17.cloned.1.call-done = f32[32,64]{1,0:T(8,128)} async-done(((f32[512,64]{1,0:T(8,128)}), f32[32,64]{1,0:T(8,128)}) %reduce-scatter.17.cloned.1.call-update) | async-done | bytes 8208 | tf_op jit(solution)/shard_map/reduce_scatter | solution.py:99
  536.3 17.2 %all_gather.22 = bf16[512,64]{1,0:T(8,128)(2,1)S(1)} all-gather(bf16[32,64]{1,0:T(8,128)(2,1)S(1)} %convert_element_type.173), channel_id=1, replica_groups=mesh['store'=8,'mp'=16] {'mp'}, dimensions={0}, use_global_device_ids=true | all-gather | bytes 69632 | tf_op jit(solution)/shard_map/all_gather | solution.py:102
  555.4 20.7 %all_to_all.82 = bf16[8,64,384]{2,1,0:T(8,128)(2,1)S(1)} all-to-all(bf16[8,64,384]{2,1,0:T(8,128)(2,1)S(1)} %bitcast.145), channel_id=1, replica_groups=mesh['store'=8,'mp'=16] {'store'}, dimensions={0} | all-to-all | bytes 786432 | tf_op jit(solution)/shard_map/all_to_all | solution.py:112
  582.9 42.6 %all_to_all.83 = bf16[256,16,384]{2,0,1:T(8,128)(2,1)} all-to-all(bf16[256,16,384]{2,0,1:T(8,128)(2,1)S(1)} %tile.11), channel_id=1, replica_groups=mesh['store'=8,'mp'=16] {'mp'}, dimensions={1} | all-to-all | bytes 6291456 | tf_op jit(solution)/shard_map/all_to_all | solution.py:14
  634.0 12.4 %all_to_all.84 = bf16[8,64,384]{2,1,0:T(8,128)(2,1)S(1)} all-to-all(bf16[8,64,384]{2,1,0:T(8,128)(2,1)S(1)} %bitcast.133), channel_id=1, replica_groups=mesh['store'=8,'mp'=16] {'store'}, dimensions={0} | all-to-all | bytes 786432 | tf_op jit(solution)/shard_map/all_to_all | solution.py:83
  649.0 67.5 %reduce-scatter.19.cloned.1.call-done = f32[32,64]{1,0:T(8,128)} async-done(((f32[512,64]{1,0:T(8,128)}), f32[32,64]{1,0:T(8,128)}) %reduce-scatter.19.cloned.1.call-update) | async-done | bytes 8208 | tf_op jit(solution)/shard_map/reduce_scatter | solution.py:99
  717.2 16.9 %all_gather.23 = bf16[512,64]{1,0:T(8,128)(2,1)S(1)} all-gather(bf16[32,64]{1,0:T(8,128)(2,1)S(1)} %convert_element_type.182), channel_id=1, replica_groups=mesh['store'=8,'mp'=16] {'mp'}, dimensions={0}, use_global_device_ids=true | all-gather | bytes 69632 | tf_op jit(solution)/shard_map/all_gather | solution.py:102
  736.1 20.7 %all_to_all.85 = bf16[8,64,384]{2,1,0:T(8,128)(2,1)S(1)} all-to-all(bf16[8,64,384]{2,1,0:T(8,128)(2,1)S(1)} %bitcast.141), channel_id=1, replica_groups=mesh['store'=8,'mp'=16] {'store'}, dimensions={0} | all-to-all | bytes 786432 | tf_op jit(solution)/shard_map/all_to_all | solution.py:112
  (155 shorter events, 101.7 us)
Async XLA Ops:
  6.5 28.8 %copy-start = (s32[8,4]{0,1:T(4,128)S(1)}, s32[8,4]{0,1:T(4,128)}, u32[]{:S(2)}) copy-start(s32[8,4]{0,1:T(4,128)} %param.13) | copy-start | bytes 388
  6.5 88.9 %all-gather.3.cloned.1.call-start = ((), (), s32[]{:S(2)}) async-start(), calls=%async_computation.17 | async-start | bytes 3538944 | tf_op jit(solution)/shard_map/all_gather | solution.py:31
  27.3 53.8 %all-to-all-start = ((bf16[256,16,384]{2,0,1:T(8,128)(2,1)}), bf16[256,16,384]{2,0,1:T(8,128)(2,1)}, u32[]{:S(2)}, u32[]{:S(2)}) async-start(bf16[256,16,384]{2,0,1:T(8,128)(2,1)} %tile.8), calls=%async_computation | async-start | bytes 6291456 | tf_op jit(solution)/shard_map/all_to_all | solution.py:14
  34.3 70.4 %all-gather.5.cloned.1.call-start = ((), (), s32[]{:S(2)}) async-start(), calls=%async_computation.18 | async-start | bytes 3538944 | tf_op jit(solution)/shard_map/all_gather | solution.py:32
  38.4 64.7 %copy-start.21 = (f32[512,12]{0,1:T(8,128)}, f32[512,12]{0,1:T(8,128)S(1)}, u32[]{:S(2)}) copy-start(f32[512,12]{0,1:T(8,128)S(1)} %get-tuple-element.6) | copy-start | bytes 73732
  38.4 152.9 %copy-start.25 = (bf16[512,12]{0,1:T(8,128)(2,1)}, bf16[512,12]{0,1:T(8,128)(2,1)S(1)}, u32[]{:S(2)}) copy-start(bf16[512,12]{0,1:T(8,128)(2,1)S(1)} %get-tuple-element.5) | copy-start | bytes 36868
  87.9 10.0 %copy-start.19 = (bf16[12,64,384]{2,1,0:T(8,128)(2,1)S(1)}, bf16[12,64,384]{2,1,0:T(8,128)(2,1)}, u32[]{:S(2)}) copy-start(bf16[12,64,384]{2,1,0:T(8,128)(2,1)} %constant_dynamic-update-slice_fusion) | copy-start | bytes 1769476
  90.3 12.9 %all-to-all-start.2 = ((bf16[8,64,384]{2,1,0:T(8,128)(2,1)}), bf16[8,64,384]{2,1,0:T(8,128)(2,1)S(1)}, u32[]{:S(2)}, u32[]{:S(2)}) async-start(bf16[8,64,384]{2,1,0:T(8,128)(2,1)} %bitcast.7), calls=%async_computation.2 | async-start | bytes 786432 | tf_op jit(solution)/shard_map/all_to_all | solution.py:83
  95.4 78.2 %reduce-scatter.13.cloned.1.call-start = ((), (), s32[]{:S(2)}) async-start(), calls=%async_computation.19 | async-start | bytes 278528 | tf_op jit(solution)/shard_map/reduce_scatter | solution.py:99
  97.9 9.2 %copy-start.20 = (bf16[12,64,384]{2,1,0:T(8,128)(2,1)}, bf16[12,64,384]{2,1,0:T(8,128)(2,1)S(1)}, u32[]{:S(2)}) copy-start(bf16[12,64,384]{2,1,0:T(8,128)(2,1)S(1)} %bitcast_dynamic-update-slice_fusion.1) | copy-start | bytes 1769476
  191.4 25.0 %copy-start.3 = (bf16[256,6144]{0,1:T(8,128)(2,1)S(1)}, bf16[256,6144]{0,1:T(8,128)(2,1)}, u32[]{:S(2)}) copy-start(bf16[256,6144]{0,1:T(8,128)(2,1)} %copy-done.2) | copy-start | bytes 9437188
  193.9 20.6 %all-to-all-start.3 = ((bf16[8,64,384]{2,1,0:T(8,128)(2,1)}), bf16[8,64,384]{2,1,0:T(8,128)(2,1)S(1)}, u32[]{:S(2)}, u32[]{:S(2)}) async-start(bf16[8,64,384]{2,1,0:T(8,128)(2,1)} %bitcast.139), calls=%async_computation.3 | async-start | bytes 786432 | tf_op jit(solution)/shard_map/all_to_all | solution.py:112
  206.8 148.0 %reduce-scatter.15.cloned.1.call-start = ((), (), s32[]{:S(2)}) async-start(), calls=%async_computation.20 | async-start | bytes 278528 | tf_op jit(solution)/shard_map/reduce_scatter | solution.py:99
  267.6 17.2 %copy-start.22 = (f32[512,12]{0,1:T(8,128)S(1)}, f32[512,12]{0,1:T(8,128)}, u32[]{:S(2)}) copy-start(f32[512,12]{0,1:T(8,128)} %copy-done.21) | copy-start | bytes 73732
  270.3 102.3 %copy-start.26 = (bf16[512,12]{0,1:T(8,128)(2,1)S(1)}, bf16[512,12]{0,1:T(8,128)(2,1)}, u32[]{:S(2)}) copy-start(bf16[512,12]{0,1:T(8,128)(2,1)} %copy-done.25) | copy-start | bytes 36868
  287.4 248.1 %reduce-scatter.17.cloned.1.call-start = ((), (), s32[]{:S(2)}) async-start(), calls=%async_computation.21 | async-start | bytes 278528 | tf_op jit(solution)/shard_map/reduce_scatter | solution.py:99
  372.6 24.4 %copy-start.7 = (bf16[256,6144]{0,1:T(8,128)(2,1)S(1)}, bf16[256,6144]{0,1:T(8,128)(2,1)}, u32[]{:S(2)}) copy-start(bf16[256,6144]{0,1:T(8,128)(2,1)} %copy-done.6) | copy-start | bytes 9437188
  448.6 16.9 %copy-start.23 = (f32[512,12]{0,1:T(8,128)S(1)}, f32[512,12]{0,1:T(8,128)}, u32[]{:S(2)}) copy-start(f32[512,12]{0,1:T(8,128)} %copy-done.21) | copy-start | bytes 73732
  451.3 102.2 %copy-start.27 = (bf16[512,12]{0,1:T(8,128)(2,1)S(1)}, bf16[512,12]{0,1:T(8,128)(2,1)}, u32[]{:S(2)}) copy-start(bf16[512,12]{0,1:T(8,128)(2,1)} %copy-done.25) | copy-start | bytes 36868
  468.1 248.4 %reduce-scatter.19.cloned.1.call-start = ((), (), s32[]{:S(2)}) async-start(), calls=%async_computation.22 | async-start | bytes 278528 | tf_op jit(solution)/shard_map/reduce_scatter | solution.py:99
  553.5 24.4 %copy-start.9 = (bf16[256,6144]{0,1:T(8,128)(2,1)S(1)}, bf16[256,6144]{0,1:T(8,128)(2,1)}, u32[]{:S(2)}) copy-start(bf16[256,6144]{0,1:T(8,128)(2,1)} %copy-done.8) | copy-start | bytes 9437188
  629.5 16.9 %copy-start.24 = (f32[512,12]{0,1:T(8,128)S(1)}, f32[512,12]{0,1:T(8,128)}, u32[]{:S(2)}) copy-start(f32[512,12]{0,1:T(8,128)} %copy-done.21) | copy-start | bytes 73732
  632.2 102.0 %copy-start.28 = (bf16[512,12]{0,1:T(8,128)(2,1)S(1)}, bf16[512,12]{0,1:T(8,128)(2,1)}, u32[]{:S(2)}) copy-start(bf16[512,12]{0,1:T(8,128)(2,1)} %copy-done.25) | copy-start | bytes 36868
  734.2 24.4 %copy-start.5 = (bf16[256,6144]{0,1:T(8,128)(2,1)S(1)}, bf16[256,6144]{0,1:T(8,128)(2,1)}, u32[]{:S(2)}) copy-start(bf16[256,6144]{0,1:T(8,128)(2,1)} %copy-done.4) | copy-start | bytes 9437188
  (14 other events, 32.5 us)
Sparse Core Ops, SparseCore 0:
  9.0 31.5 all-gather.2
  42.3 27.6 all-gather.4
  104.8 68.7 reduce-scatter.12
  287.5 67.2 reduce-scatter.14
  468.2 67.2 reduce-scatter.16
  649.1 67.2 reduce-scatter.18
